TPU v7x, 32 devices: a whole 2x2x4 slice. The times are simulated.
32 devices in a mesh: freq: 4 (over x, core), tm: 8 (over z, y).
Axes of the slice: x: 2, y: 2, z: 4, core: 2. Of those that a mesh axis runs over, the one named last changes fastest.
Arguments:
- visibilities: float32 [8, 8, 1024], P('freq', None, 'tm'), may hold values from -6 to 6
- coherencies: bfloat16 [8, 8, 8, 1024], P('freq', None, None, 'tm'), may hold values from -2.09375 to 2.09375
- pairs: int32 [2, 1024], P(None, 'tm'), may hold values from 0 to 511, as said below
- gains_start: float32 [8, 8, 8, 512], P('freq'), may hold values from -0.9 to 1.9
- duals_start: float32 [8, 8, 8, 512], P('freq'), may hold values from -12 to 12
- poly_start: float32 [4, 8, 8, 512], replicated, may hold values from -0.6 to 1.6
Outputs:
- gains: float32 [8, 8, 8, 512], P('freq')
- duals: float32 [8, 8, 8, 512], P('freq')
- polynomial: float32 [4, 8, 8, 512], replicated
Inputs may be any that keep to these rules, and one draw needn't show every extreme that they name: `pairs`: each row names two different stations.
All inputs are finite; a program needn't handle non-finite values.
Results may differ from a plain program's by a relative error of at most 0.0003.
Values sent between devices are 32-bit elements; how exact they have to be, the bound alone decides.
A program may use at most 64 MiB of HBM per device.

v0:
```python
from functools import partial

import jax
import jax.numpy as jnp
from jax import lax
from jax.sharding import PartitionSpec as P

ITERS = 2


RHO = 16.0
HIGHEST = lax.Precision.HIGHEST


def split(block):
    return ([block[i] for i in range(4)], [block[i + 4] for i in range(4)])


def join(matrix):
    return jnp.stack(matrix[0] + matrix[1])


def adjoint(matrix):
    real_part, imag_part = matrix
    return (
        [real_part[0], real_part[2], real_part[1], real_part[3]],
        [-imag_part[0], -imag_part[2], -imag_part[1], -imag_part[3]],
    )


def product(left, right):
    left_real, left_imag = left
    right_real, right_imag = right
    out_real = []
    out_imag = []
    for row in range(2):
        for column in range(2):
            first = 2 * row
            out_real.append(
                left_real[first] * right_real[column]
                - left_imag[first] * right_imag[column]
                + left_real[first + 1] * right_real[column + 2]
                - left_imag[first + 1] * right_imag[column + 2]
            )
            out_imag.append(
                left_real[first] * right_imag[column]
                + left_imag[first] * right_real[column]
                + left_real[first + 1] * right_imag[column + 2]
                + left_imag[first + 1] * right_real[column + 2]
            )
    return (out_real, out_imag)


def normal(matrix):
    real_part, imag_part = matrix
    top_left = real_part[0] ** 2 + imag_part[0] ** 2 + real_part[1] ** 2 + imag_part[1] ** 2
    bottom_right = real_part[2] ** 2 + imag_part[2] ** 2 + real_part[3] ** 2 + imag_part[3] ** 2
    cross_real = (
        real_part[0] * real_part[2]
        + imag_part[0] * imag_part[2]
        + real_part[1] * real_part[3]
        + imag_part[1] * imag_part[3]
    )
    cross_imag = (
        imag_part[0] * real_part[2]
        - real_part[0] * imag_part[2]
        + imag_part[1] * real_part[3]
        - real_part[1] * imag_part[3]
    )
    return jnp.stack([top_left, bottom_right, cross_real, cross_imag])


def data_sums(gains, coherencies, visibilities, pairs):
    jones_first = split(jnp.take(gains, pairs[0], axis=2))
    jones_second = split(jnp.take(gains, pairs[1], axis=2))
    skymodel = split(coherencies.astype(jnp.float32))
    left = product(jones_first, skymodel)
    right = product(skymodel, adjoint(jones_second))
    model = jnp.sum(join(product(left, adjoint(jones_second))), axis=1)
    residual = split((visibilities - model)[:, None, :])
    first_terms = jnp.concatenate([join(product(residual, adjoint(right))), normal(right)], axis=0)
    second_terms = jnp.concatenate(
        [join(product(adjoint(residual), left)), normal(adjoint(left))], axis=0
    )
    terms = jnp.concatenate([first_terms, second_terms], axis=2)
    stations = jnp.concatenate([pairs[0], pairs[1]])
    flat = terms.reshape(-1, terms.shape[2]).T
    summed = jax.ops.segment_sum(flat, stations, num_segments=gains.shape[2])
    return summed.T.reshape(12, gains.shape[1], gains.shape[2])


def update(gains, duals, prior, sums, damping):
    direction = split(sums[:8] - duals - RHO * (gains - prior))
    top_left, bottom_right, cross_real, cross_imag = (sums[8], sums[9], sums[10], sums[11])
    shift = damping * 0.5 * (top_left + bottom_right) + RHO
    upper = top_left + shift
    lower = bottom_right + shift
    determinant = upper * lower - cross_real * cross_real - cross_imag * cross_imag
    zeros = jnp.zeros_like(determinant)
    inverse = (
        [
            lower / determinant,
            -cross_real / determinant,
            -cross_real / determinant,
            upper / determinant,
        ],
        [zeros, -cross_imag / determinant, cross_imag / determinant, zeros],
    )
    return gains + join(product(direction, inverse))


def basis_weights(count):
    position = (2.0 * jnp.arange(count).astype(jnp.float32) + 1.0) / count - 1.0
    basis = jnp.stack(
        [
            jnp.ones_like(position),
            position,
            1.5 * position * position - 0.5,
            2.5 * position * position * position - 1.5 * position,
        ],
        axis=1,
    )
    gram = jnp.dot(basis.T, basis, precision=HIGHEST)
    factor = jnp.linalg.cholesky(gram)
    weights = jax.scipy.linalg.cho_solve((factor, True), basis.T)
    return (basis, weights)


def shards(visibilities, coherencies, pairs, gains_start, duals_start, poly_start):
    channels = gains_start.shape[0]
    offset = lax.axis_index("freq") * channels
    basis, weights = basis_weights(channels * lax.axis_size("freq"))
    local_basis = lax.dynamic_slice_in_dim(basis, offset, channels, 0)
    local_weights = lax.dynamic_slice_in_dim(weights, offset, channels, 1)
    channel_sums = jax.vmap(data_sums, in_axes=(0, 0, 0, None))
    gains, duals = (gains_start, duals_start)
    prior = jnp.einsum("fj,jcks->fcks", local_basis, poly_start, precision=HIGHEST)
    for inner in range(ITERS):
        local_terms = channel_sums(gains, coherencies, visibilities, pairs)
        sums = lax.psum(local_terms, "tm")
        gains = jax.vmap(partial(update, damping=12.0 * 0.5**inner))(gains, duals, prior, sums)
    mixed = gains + duals / RHO
    partial_fit = jnp.einsum("jf,fcks->jcks", local_weights, mixed, precision=HIGHEST)
    polynomial = lax.psum(partial_fit, "freq")
    prior = jnp.einsum("fj,jcks->fcks", local_basis, polynomial, precision=HIGHEST)
    duals = duals + RHO * (gains - prior)
    return (gains, duals, polynomial)


def solution(mesh):
    placed = (
        P("freq", None, "tm"),
        P("freq", None, None, "tm"),
        P(None, "tm"),
        P("freq", None, None, None),
        P("freq", None, None, None),
        P(),
    )
    return jax.shard_map(
        shards,
        mesh=mesh,
        in_specs=placed,
        out_specs=(P("freq", None, None, None), P("freq", None, None, None), P()),
        check_vma=False,
    )
```

profile of v0, /device:TPU:0, one launch (start us, length us, event | category | flops | bytes accessed | tf_op | source)
XLA Modules:
  0.0 250.6 jit_solution(10916335076422849878)
XLA Ops:
  7.2 0.8 compare_and_fusion.1
  8.0 3.5 %copy.795 = f32[2,8,8,512]{2,1,3,0:T(8,128)} copy(f32[2,8,8,512]{3,2,1,0:T(8,128)} %param.11) | data formatting | bytes 524288 | tf_op args[3]
  11.5 2.9 %gather_fusion.1 = f32[128,2,8,8]{3,2,1,0:T(8,128)S(1)} fusion(f32[2,8,8,512]{2,1,3,0:T(8,128)} %copy.795, s32[1024]{0:T(1024)S(1)} %pad_clamp_fusion), kind=kCustom, calls=%fused_computation.1.clone | custom fusion | bytes 131584 | tf_op jit(solution)/shard_map/vmap(jit(_take))/gather | solution.py:75
  14.4 0.4 copy.799
  14.8 2.9 %gather_fusion = f32[128,2,8,8]{3,2,1,0:T(8,128)S(1)} fusion(f32[2,8,8,512]{2,1,3,0:T(8,128)} %copy.795, s32[1024]{0:T(1024)S(1)} %pad_clamp_fusion.1), kind=kCustom, calls=%fused_computation.clone | custom fusion | bytes 131584 | tf_op jit(solution)/shard_map/vmap(jit(_take))/gather | solution.py:74
  17.7 0.4 copy.796
  18.4 0.2 copy.870
  18.6 0.2 copy.801
  20.3 0.1 copy.818
  20.5 0.1 broadcast.1350.clone
  20.6 8.3 %scatter_fusion = f32[2,512,96]{2,0,1:T(2,128)S(1)} fusion(f32[2,512,96]{2,0,1:T(2,128)S(1)} %broadcast.1350.clone, s32[256]{0:T(256)S(1)} %pad_add_fusion, f32[256,2,96]{2,1,0:T(2,128)S(1)} %copy.818), kind=kCustom, calls=%fused_computation.4 | custom fusion | flops 49152 | bytes 590848 | tf_op jit(solution)/shard_map/vmap()/scatter-add | solution.py:88
  29.0 0.2 copy.819
  29.2 0.8 copy.820
  30.2 0.2 fusion.63
  30.4 0.1 copy.853
  30.5 0.4 cholesky.16
  30.9 0.6 compare_reduce_fusion
  31.5 0.6 fusion.31
  32.2 0.3 custom-call.10
  32.5 1.2 fusion.2
  33.8 70.9 %all-reduce.4.cloned.1.call-done = f32[2,12,8,512]{3,2,0,1:T(8,128)} async-done(((f32[2,12,8,512]{3,2,0,1:T(8,128)}), f32[2,12,8,512]{3,2,0,1:T(8,128)}) %all-reduce.4.cloned.1.call-update) | async-done | bytes 393232 | tf_op jit(solution)/shard_map/psum | solution.py:140
  104.7 1.1 fusion.5
  105.8 0.8 constant_dynamic-update-slice_fusion.31
  106.7 0.8 constant_dynamic-update-slice_fusion.30
  107.7 2.6 %copy.826 = f32[2,8,8,512]{2,1,3,0:T(8,128)} copy(f32[2,8,8,512]{3,2,0,1:T(8,128)S(1)} %bitcast_add_fusion.1) | data formatting | bytes 524288 | tf_op jit(solution)/shard_map/vmap()/add | solution.py:109
  110.3 2.9 %gather_fusion.2 = f32[128,2,8,8]{3,2,1,0:T(8,128)S(1)} fusion(f32[2,8,8,512]{2,1,3,0:T(8,128)} %copy.826, s32[1024]{0:T(1024)S(1)} %pad_clamp_fusion.1), kind=kCustom, calls=%fused_computation.2.clone | custom fusion | bytes 131584 | tf_op jit(solution)/shard_map/vmap(jit(_take))/gather | solution.py:74
  113.2 3.8 %gather_fusion.3 = f32[128,2,8,8]{3,2,1,0:T(8,128)} fusion(f32[2,8,8,512]{2,1,3,0:T(8,128)} %copy.826, s32[1024]{0:T(1024)S(1)} %pad_clamp_fusion), kind=kCustom, calls=%fused_computation.3.clone | custom fusion | bytes 131584 | tf_op jit(solution)/shard_map/vmap(jit(_take))/gather | solution.py:75
  117.0 0.4 copy.827
  117.4 1.6 copy.829
  119.2 0.2 copy.871
  120.9 0.1 copy.848
  121.1 0.1 broadcast.1350
  121.2 8.3 %scatter_fusion.1 = f32[2,512,96]{2,0,1:T(2,128)S(1)} fusion(f32[2,512,96]{2,0,1:T(2,128)S(1)} %broadcast.1350, s32[256]{0:T(256)S(1)} %pad_add_fusion, f32[256,2,96]{2,1,0:T(2,128)S(1)} %copy.848), kind=kCustom, calls=%fused_computation.5 | custom fusion | flops 49152 | bytes 590848 | tf_op jit(solution)/shard_map/vmap()/scatter-add | solution.py:88
  129.6 0.2 copy.849
  129.8 0.8 copy.850
  130.6 0.2 all-reduce.8.cloned.1.call-start
  130.8 0.2 fusion.32
  131.0 0.2 fusion.34
  131.2 70.3 %all-reduce.6.cloned.1.call-done = f32[2,12,8,512]{3,2,0,1:T(8,128)} async-done(((f32[2,12,8,512]{3,2,0,1:T(8,128)}), f32[2,12,8,512]{3,2,0,1:T(8,128)}) %all-reduce.6.cloned.1.call-update) | async-done | bytes 393232 | tf_op jit(solution)/shard_map/psum | solution.py:140
  201.5 1.1 fusion.4
  202.6 0.8 constant_dynamic-update-slice_fusion.63
  203.5 0.8 constant_dynamic-update-slice_fusion.62
  204.5 2.1 fusion.8
  206.6 0.7 copy.859
  207.4 31.9 %all-reduce.8.cloned.1.call-done = f32[4,8,8,512]{3,0,2,1:T(4,128)} async-done(((f32[4,8,8,512]{3,0,2,1:T(4,128)}), f32[4,8,8,512]{3,0,2,1:T(4,128)}) %all-reduce.8.cloned.1.call-update) | async-done | bytes 524304 | tf_op jit(solution)/shard_map/psum | solution.py:144
  239.2 2.0 fusion.38
  241.4 0.7 copy.860
  242.1 2.0 copy.861
  (131 shorter events, 3.7 us)
Async XLA Ops:
  7.2 25.4 %copy-start = (f32[4,8,8,512]{3,2,1,0:T(8,128)S(1)}, f32[4,8,8,512]{3,2,1,0:T(8,128)}, u32[]{:S(2)}) copy-start(f32[4,8,8,512]{3,2,1,0:T(8,128)} %param.13) | copy-start | bytes 1572868
  7.2 10.9 %copy-start.3 = (bf16[2,8,8,128]{3,2,1,0:T(8,128)(2,1)S(1)}, bf16[2,8,8,128]{3,2,1,0:T(8,128)(2,1)}, u32[]{:S(2)}) copy-start(bf16[2,8,8,128]{3,2,1,0:T(8,128)(2,1)} %param.9) | copy-start | bytes 98308
  7.2 97.5 %all-reduce.4.cloned.1.call-start = ((), (), s32[]{:S(2)}) async-start(), calls=%async_computation | async-start | bytes 786432 | tf_op jit(solution)/shard_map/psum | solution.py:140
  8.0 10.6 %copy-start.4 = (f32[2,8,128]{2,1,0:T(8,128)S(1)}, f32[2,8,128]{2,1,0:T(8,128)}, u32[]{:S(2)}) copy-start(f32[2,8,128]{2,1,0:T(8,128)} %param.8) | copy-start | bytes 24580
  11.5 7.5 %copy-start.5 = (s32[2,128]{1,0:T(2,128)S(1)}, s32[2,128]{1,0:T(2,128)}, u32[]{:S(2)}) copy-start(s32[2,128]{1,0:T(2,128)} %param.10) | copy-start | bytes 3076
  18.9 85.8 %copy-start.1 = (f32[2,8,8,512]{3,2,1,0:T(8,128)S(1)}, f32[2,8,8,512]{3,2,1,0:T(8,128)}, u32[]{:S(2)}) copy-start(f32[2,8,8,512]{3,2,1,0:T(8,128)} %param.12) | copy-start | bytes 786436
  18.9 85.8 %copy-start.2 = (f32[2,8,8,512]{3,2,1,0:T(8,128)S(1)}, f32[2,8,8,512]{3,2,1,0:T(8,128)}, u32[]{:S(2)}) copy-start(f32[2,8,8,512]{3,2,1,0:T(8,128)} %param.11) | copy-start | bytes 786436
  30.0 171.6 %all-reduce.6.cloned.1.call-start = ((), (), s32[]{:S(2)}) async-start(), calls=%async_computation.1 | async-start | bytes 786432 | tf_op jit(solution)/shard_map/psum | solution.py:140
  130.6 108.7 %all-reduce.8.cloned.1.call-start = ((), (), s32[]{:S(2)}) async-start(), calls=%async_computation.2 | async-start | bytes 1048576 | tf_op jit(solution)/shard_map/psum | solution.py:144
Sparse Core Ops, SparseCore 0:
  30.1 74.5 all-reduce.3
  130.7 70.8 all-reduce.5
  206.8 32.4 all-reduce.7
where the time goes:
time: 251 us
  waiting for transfers between devices  173 us (69%)
  local copies, waits for them, and re-layouts  30 us (12%)
  other arithmetic  26.6 us (11%)
  between operations  14.6 us (6%)
  matrix products  5.93 us (2%)
    psum x2, waiting for transfers between devices, shards(): sums = lax.psum(local_terms, 'tm')  141 us
    psum x1, waiting for transfers between devices, shards(): polynomial = lax.psum(partial_fit, 'freq')  31.9 us
    scatter-add x2, other arithmetic, data_sums(): summed = jax.ops.segment_sum(flat, stations, num_segments=gains.shape[2])  16.7 us
    gather x4, local copies, waits for them, and re-layouts, data_sums(): jones_second = split(jnp.take(gains, pairs[1], axis=2))  8.74 us
    unnamed x19, local copies, waits for them, and re-layouts  7.63 us
    gather x4, local copies, waits for them, and re-layouts, data_sums(): jones_first = split(jnp.take(gains, pairs[0], axis=2))  6.57 us
  transfers between devices with their start and end apart: 3, of which 3 were waited for; matrix products, arithmetic and copies ran while one was open for 2% of the time, Pallas kernels for 0%

commit v1 on v0

v1 whole, which is shorter than its diff:
```python
from functools import partial

import jax
import jax.numpy as jnp
import numpy as np
from jax import lax
from jax.experimental import pallas as pl
from jax.experimental.pallas import tpu as pltpu
from jax.sharding import PartitionSpec as P

ITERS = 2
RHO = 16.0
LANES = 128
OUTER = 4


def split(block):
    return ([block[i] for i in range(4)], [block[i + 4] for i in range(4)])


def product(left, right):
    lr, li = left
    rr, ri = right
    out_real, out_imag = [], []
    for row in range(2):
        for col in range(2):
            a, b = 2 * row, 2 * row + 1
            out_real.append(lr[a] * rr[col] - li[a] * ri[col] + lr[b] * rr[col + 2] - li[b] * ri[col + 2])
            out_imag.append(lr[a] * ri[col] + li[a] * rr[col] + lr[b] * ri[col + 2] + li[b] * rr[col + 2])
    return (out_real, out_imag)


def product_right_adjoint(left, right):
    lr, li = left
    rr, ri = right
    out_real, out_imag = [], []
    for row in range(2):
        for col in range(2):
            a, b, c, d = 2 * row, 2 * row + 1, 2 * col, 2 * col + 1
            out_real.append(lr[a] * rr[c] + li[a] * ri[c] + lr[b] * rr[d] + li[b] * ri[d])
            out_imag.append(li[a] * rr[c] - lr[a] * ri[c] + li[b] * rr[d] - lr[b] * ri[d])
    return (out_real, out_imag)


def product_left_adjoint(left, right):
    lr, li = left
    rr, ri = right
    out_real, out_imag = [], []
    for row in range(2):
        for col in range(2):
            a, b, c, d = row, row + 2, col, col + 2
            out_real.append(lr[a] * rr[c] + li[a] * ri[c] + lr[b] * rr[d] + li[b] * ri[d])
            out_imag.append(lr[a] * ri[c] - li[a] * rr[c] + lr[b] * ri[d] - li[b] * rr[d])
    return (out_real, out_imag)


def normal(r, i, rows):
    (a, b), (c, d) = rows
    top = r[a] * r[a] + i[a] * i[a] + r[b] * r[b] + i[b] * i[b]
    bottom = r[c] * r[c] + i[c] * i[c] + r[d] * r[d] + i[d] * i[d]
    real = r[a] * r[c] + i[a] * i[c] + r[b] * r[d] + i[b] * i[d]
    imag = i[a] * r[c] - r[a] * i[c] + i[b] * r[d] - r[b] * i[d]
    return top, bottom, real, imag


def basis_weights(count):
    x = (2.0 * np.arange(count, dtype=np.float64) + 1.0) / count - 1.0
    basis = np.stack([np.ones_like(x), x, 1.5 * x * x - 0.5, 2.5 * x * x * x - 1.5 * x], axis=1)
    return np.linalg.solve(basis.T @ basis, basis.T)


def halves(value):
    high = value.astype(jnp.bfloat16)
    return high, (value - high.astype(jnp.float32)).astype(jnp.bfloat16)


def kernel(cfg, vis_ref, coh_ref, pairs_ref, gains_ref, duals_ref, poly_ref,
           gains_out, duals_out, poly_out,
           data, hot, terms, jones, mixed,
           tm_send, tm_recv, fq_send, fq_recv):
    F, K, S, nt, nf, inner, chunks, terms_poly = cfg
    CH = S // chunks
    FK = F * 8 * K
    tm = lax.axis_index("tm")
    fq = lax.axis_index("freq")
    z, y = tm // inner, tm % inner
    partner = fq + 1 - 2 * (fq % 2)

    def tm_at(dz, dy):
        return ((z + dz) % OUTER) * inner + (y + dy) % inner

    head = 8 + F * 8
    data[tm, 0:2, :] = pairs_ref[...].astype(jnp.float32)
    data[tm, 8:head, :] = vis_ref[...].reshape(F * 8, LANES)
    data[tm, head:, :] = coh_ref[...].astype(jnp.float32).reshape(F * 8 * K, LANES)

    barrier = pltpu.get_barrier_semaphore()
    peers = [{"tm": tm_at(d, 0)} for d in range(1, OUTER)]
    peers += [{"tm": tm_at(0, e)} for e in range(1, inner)]
    peers += [{"freq": partner}]
    peers += [{"freq": (fq + 2 * d) % nf} for d in range(1, nf // 2)]
    for peer in peers:
        pl.semaphore_signal(barrier, inc=1, device_id=peer, device_id_type=pl.DeviceIdType.MESH)

    def load_gains(gains):
        high, low = halves(gains)
        jones[0:FK, :] = high
        jones[FK : 2 * FK, :] = low

    load_gains(gains_ref[...].reshape(FK, S))
    pl.semaphore_wait(barrier, len(peers))

    def tm_copy(block, slot, device):
        return pltpu.make_async_remote_copy(
            src_ref=data.at[block], dst_ref=data.at[block],
            send_sem=tm_send.at[slot], recv_sem=tm_recv.at[block],
            device_id={"tm": device}, device_id_type=pl.DeviceIdType.MESH)

    sends = []

    def send(block, device):
        copy = tm_copy(block, len(sends), device)
        copy.start()
        sends.append(copy)

    for e in range(1, inner):
        send(tm, tm_at(0, e))
    for d in (1, 3, 2):
        send(tm, tm_at(d, 0))

    stations = lax.broadcasted_iota(jnp.int32, (S, LANES), 0).astype(jnp.float32)

    def columns(block, half):
        return pl.ds(pl.multiple_of(block * 2 * LANES + half * LANES, LANES), LANES)

    def make_hot(block):
        for half in range(2):
            row = data[block, half : half + 1, :]
            hot[:, columns(block, half)] = jnp.where(stations == row, 1.0, 0.0).astype(jnp.bfloat16)

    def rows_sums(block):
        both = pl.ds(pl.multiple_of(block * 2 * LANES, 2 * LANES), 2 * LANES)
        taken = jnp.dot(jones[...], hot[:, both], preferred_element_type=jnp.float32)
        taken = taken[:FK] + taken[FK:]
        for f in range(F):
            base = f * 8 * K
            first = split([taken[base + c * K : base + (c + 1) * K, :LANES] for c in range(8)])
            second = split([taken[base + c * K : base + (c + 1) * K, LANES:] for c in range(8)])
            start = head + base
            sky = split([data[block, start + c * K : start + (c + 1) * K, :] for c in range(8)])
            left = product(first, sky)
            right = product_right_adjoint(sky, second)
            model = product_right_adjoint(left, second)
            model = model[0] + model[1]
            residual = []
            for c in range(8):
                seen = data[block, 8 + f * 8 + c : 8 + f * 8 + c + 1, :]
                residual.append(jnp.broadcast_to(seen - jnp.sum(model[c], axis=0, keepdims=True), (K, LANES)))
            residual = split(residual)
            ends = []
            out = product_right_adjoint(residual, right)
            ends.append(out[0] + out[1] + list(normal(right[0], right[1], ((0, 1), (2, 3)))))
            out = product_left_adjoint(residual, left)
            top, bottom, real, imag = normal(left[0], left[1], ((0, 2), (1, 3)))
            ends.append(out[0] + out[1] + [top, bottom, real, -imag])
            for half in range(2):
                high, low = halves(jnp.concatenate(ends[half], axis=0))
                terms[f * 12 * K : (f + 1) * 12 * K, columns(block, half)] = high
                terms[(F + f) * 12 * K : (F + f + 1) * 12 * K, columns(block, half)] = low

    def basis_at(f):
        channel = (fq * F + f).astype(jnp.float32)
        x = (2.0 * channel + 1.0) / (F * nf) - 1.0
        return [None, x, 1.5 * x * x - 0.5, 2.5 * x * x * x - 1.5 * x]

    bases = [basis_at(f) for f in range(F)]

    def from_basis(f, coefficients):
        total = coefficients[0]
        for j in range(1, terms_poly):
            total = total + bases[f][j] * coefficients[j]
        return total

    def update(source, damping, chunk):
        lanes = slice(chunk * CH, (chunk + 1) * CH)
        sums = lax.dot_general(terms[...], hot[lanes, :], (((1,), (1,)), ((), ())),
                               preferred_element_type=jnp.float32)
        half = F * 12 * K
        sums = sums[:half] + sums[half:]
        for f in range(F):
            part = [sums[(f * 12 + c) * K : (f * 12 + c + 1) * K] for c in range(12)]
            old, step = [], []
            for c in range(8):
                prior = from_basis(f, [poly_ref[j, c, :, lanes] for j in range(terms_poly)])
                gain = source[f, c, :, lanes]
                old.append(gain)
                step.append(part[c] - duals_ref[f, c, :, lanes] - RHO * (gain - prior))
            top, bottom, real, imag = part[8:]
            shift = damping * 0.5 * (top + bottom) + RHO
            upper, lower = top + shift, bottom + shift
            scale = 1.0 / (upper * lower - real * real - imag * imag)
            a, d, br, bi = lower * scale, upper * scale, -real * scale, -imag * scale
            sr, si = split(step)
            for row in range(2):
                p, q = 2 * row, 2 * row + 1
                gains_out[f, p, :, lanes] = old[p] + sr[p] * a + sr[q] * br + si[q] * bi
                gains_out[f, p + 4, :, lanes] = old[p + 4] + si[p] * a + si[q] * br - sr[q] * bi
                gains_out[f, q, :, lanes] = old[q] + sr[p] * br - si[p] * bi + sr[q] * d
                gains_out[f, q + 4, :, lanes] = old[q + 4] + si[p] * br + sr[p] * bi + si[q] * d

    def arrived(block):
        tm_copy(block, 0, tm).wait_recv()

    make_hot(tm)
    rows_sums(tm)
    for dz in (0, 1, 3, 2):
        if dz:
            block = tm_at(dz, 0)
            arrived(block)
            for e in range(1, inner):
                send(block, tm_at(0, e))
            make_hot(block)
            rows_sums(block)
    for dz in (0, 1, 3, 2):
        for e in range(1, inner):
            block = tm_at(dz, e)
            arrived(block)
            make_hot(block)
            rows_sums(block)

    for chunk in range(chunks):
        update(gains_ref, 12.0, chunk)
    for inner_step in range(1, ITERS):
        load_gains(gains_out[...].reshape(FK, S))

        @pl.loop(0, nt)
        def _(block):
            rows_sums(block)

        if inner_step < ITERS - 1:
            for chunk in range(chunks):
                update(gains_out, 12.0 * 0.5**inner_step, chunk)

    def fq_copy(owner, chunk, slot, device):
        return pltpu.make_async_remote_copy(
            src_ref=mixed.at[owner, chunk], dst_ref=mixed.at[owner, chunk],
            send_sem=fq_send.at[slot, chunk], recv_sem=fq_recv.at[owner, chunk],
            device_id={"freq": device}, device_id_type=pl.DeviceIdType.MESH)

    fq_sends = []

    def fq_start(owner, chunk, slot, device):
        copy = fq_copy(owner, chunk, slot, device)
        copy.start()
        fq_sends.append(copy)

    def fq_push(chunk):
        for d in range(1, nf // 2):
            fq_start(fq, chunk, d, (fq + 2 * d) % nf)
        fq_start(fq, chunk, 0, partner)

    for chunk in range(chunks):
        lanes = slice(chunk * CH, (chunk + 1) * CH)
        update(gains_out, 12.0 * 0.5 ** (ITERS - 1), chunk)
        value = gains_out[:, :, :, lanes] + duals_ref[:, :, :, lanes] * (1.0 / RHO)
        mixed[fq, chunk] = value.reshape(FK, CH)
        fq_push(chunk)

    weights = basis_weights(F * nf)
    for chunk in range(chunks):
        for d in range(1, nf // 2):
            owner = (fq - 2 * d + nf) % nf
            fq_copy(owner, chunk, 0, partner).wait_recv()
            fq_start(owner, chunk, nf // 2 + d, partner)
    for chunk in range(chunks):
        lanes = slice(chunk * CH, (chunk + 1) * CH)
        fq_copy(partner, chunk, 0, partner).wait_recv()
        for d in range(1, nf // 2):
            owner = (partner - 2 * d + nf) % nf
            fq_copy(owner, chunk, 0, partner).wait_recv()
        for c in range(8):
            rows = [mixed[n // F, chunk, ((n % F) * 8 + c) * K : ((n % F) * 8 + c + 1) * K, :] for n in range(nf * F)]
            coefficients = []
            for j in range(terms_poly):
                total = float(weights[j, 0]) * rows[0]
                for n in range(1, nf * F):
                    total = total + float(weights[j, n]) * rows[n]
                poly_out[j, c, :, lanes] = total
                coefficients.append(total)
            for f in range(F):
                prior = from_basis(f, coefficients)
                duals_out[f, c, :, lanes] = duals_ref[f, c, :, lanes] + RHO * (gains_out[f, c, :, lanes] - prior)
    for copy in sends + fq_sends:
        copy.wait_send()


def solution(mesh):
    nt, nf = mesh.shape["tm"], mesh.shape["freq"]

    def shards(visibilities, coherencies, pairs, gains_start, duals_start, poly_start):
        F, _, K, S = gains_start.shape
        inner = nt // OUTER
        chunks = 2
        FK = F * 8 * K
        cfg = (F, K, S, nt, nf, inner, chunks, poly_start.shape[0])
        like = lambda x: jax.ShapeDtypeStruct(x.shape, jnp.float32)
        vmem = pl.BlockSpec(memory_space=pltpu.VMEM)
        return pl.pallas_call(
            partial(kernel, cfg),
            out_shape=(like(gains_start), like(duals_start), like(poly_start)),
            in_specs=[vmem] * 6,
            out_specs=(vmem,) * 3,
            scratch_shapes=[
                pltpu.VMEM((nt, 8 + F * 8 + F * 8 * K, LANES), jnp.float32),
                pltpu.VMEM((S, nt * 2 * LANES), jnp.bfloat16),
                pltpu.VMEM((2 * F * 12 * K, nt * 2 * LANES), jnp.bfloat16),
                pltpu.VMEM((2 * FK, S), jnp.bfloat16),
                pltpu.VMEM((nf, chunks, FK, S // chunks), jnp.float32),
                pltpu.SemaphoreType.DMA((nt,)),
                pltpu.SemaphoreType.DMA((nt,)),
                pltpu.SemaphoreType.DMA((nf + 1, chunks)),
                pltpu.SemaphoreType.DMA((nf, chunks)),
            ],
            compiler_params=pltpu.CompilerParams(collective_id=0, has_side_effects=True,
                                                 vmem_limit_bytes=60 * 2**20),
        )(visibilities, coherencies, pairs, gains_start, duals_start, poly_start)

    placed = (
        P("freq", None, "tm"),
        P("freq", None, None, "tm"),
        P(None, "tm"),
        P("freq", None, None, None),
        P("freq", None, None, None),
        P(),
    )
    return jax.shard_map(
        shards,
        mesh=mesh,
        in_specs=placed,
        out_specs=(P("freq", None, None, None), P("freq", None, None, None), P()),
        check_vma=False,
    )
```

time: 251 us -> 36.7 us (0.15)
  waiting for transfers between devices: 173 us -> 0 us
  Pallas kernels: 0 us -> 32.5 us
  local copies, waits for them, and re-layouts: 30 us -> 3.25 us
  other arithmetic: 26.6 us -> 0 us
  between operations: 14.6 us -> 0.66 us
  matrix products: 5.93 us -> 0 us
    psum x3 -> x0, waiting for transfers between devices: 173 us -> none  [the longest x2 141 us: shards(): sums = lax.psum(local_terms, 'tm')]
    pallas_call x0 -> x1, Pallas kernels: none -> 32.5 us  [shards(): pl.pallas_call(partial(kernel, cfg), out_shape=(like(gains_start), like(d...]
    scatter-add x2 -> x0, other arithmetic: 16.7 us -> none  [data_sums(): summed = jax.ops.segment_sum(flat, stations, num_segments=gains.shape[2])]
    gather x8 -> x0, local copies, waits for them, and re-layouts: 15.3 us -> none  [the longest x4 8.74 us: data_sums(): jones_second = split(jnp.take(gains, pairs[1], axis=2))]
    dot_general x4 -> x0, matrix products: 5.54 us -> none  [the longest x1 2.1 us: shards(): jnp.einsum('jf,fcks->jcks', local_weights, mixed, precision=HIGHEST)]
    unnamed x19 -> x7, local copies, waits for them, and re-layouts: 7.63 us -> 3.25 us
    unnamed x54 -> x0, other arithmetic: 4.19 us -> none
    add x1 -> x0, local copies, waits for them, and re-layouts: 2.62 us -> none  [update(): return gains + join(product(direction, inverse))]
  transfers between devices with their start and end apart: 3 -> 0, of which waited for: 3 -> 0; matrix products, arithmetic and copies ran while one was open for 2% -> 0% of each run, Pallas kernels for 0% -> 0%
where the time goes in v1:
time: 36.7 us; the launch traced here: 36.4 us
  Pallas kernels  32.5 us (89%)
  local copies, waits for them, and re-layouts  3.25 us (9%)
  between operations  0.66 us (2%)
    pallas_call x1, Pallas kernels, shards(): pl.pallas_call(partial(kernel, cfg), out_shape=(like(gains_start), like(d...  32.5 us
    unnamed x7, local copies, waits for them, and re-layouts  3.25 us

profile of v1, /device:TPU:0, one launch (start us, length us, event | category | flops | bytes accessed | tf_op | source)
XLA Modules:
  0.0 36.4 jit_solution(14221250938840564407)
XLA Ops:
  0.6 32.5 %shard_map.85 = (f32[2,8,8,512]{3,2,1,0:T(8,128)}, f32[2,8,8,512]{3,2,1,0:T(8,128)}, f32[4,8,8,512]{3,2,1,0:T(8,128)}) custom-call(f32[2,8,128]{2,1,0:T(8,128)} %vis_ref.1, bf16[2,8,8,128]{3,2,1,0:T(8,128)(2,1)} %coh_ref.1, s32[2,128]{1,0:T(2,128)} %pairs_ref.1, f32[2,8,8,512]{3,2,1,0:T(8,128)} %gains_ref.1, f32[2,8,8,512]{3,2,1,0:T(8,128)} %duals_ref.1, ...), custom_call_target="tpu_custom_call" | custom-call | tf_op jit(solution)/shard_map/pallas_call | solution.py:308
  33.2 0.0 copy-start.1
  33.2 0.0 copy-start
  33.2 1.7 %copy.12 = f32[2,8,8,512]{3,2,1,0:T(8,128)} copy(f32[2,8,8,512]{3,2,1,0:T(8,128)} %get-tuple-element.6) | data formatting | bytes 524288
  34.9 0.0 copy-done.1
  34.9 0.7 %copy.13 = f32[2,8,8,512]{3,2,1,0:T(8,128)} copy(f32[2,8,8,512]{3,2,1,0:T(8,128)S(1)} %copy-done.1) | data formatting | bytes 524288
  35.6 0.0 copy-done
  35.6 0.8 %copy.14 = f32[4,8,8,512]{3,2,1,0:T(8,128)} copy(f32[4,8,8,512]{3,2,1,0:T(8,128)S(1)} %copy-done) | data formatting | bytes 1048576
Async XLA Ops:
  33.2 1.8 %copy-start.1 = (f32[2,8,8,512]{3,2,1,0:T(8,128)S(1)}, f32[2,8,8,512]{3,2,1,0:T(8,128)}, u32[]{:S(2)}) copy-start(f32[2,8,8,512]{3,2,1,0:T(8,128)} %get-tuple-element.7) | copy-start | bytes 786436
  33.2 2.5 %copy-start = (f32[4,8,8,512]{3,2,1,0:T(8,128)S(1)}, f32[4,8,8,512]{3,2,1,0:T(8,128)}, u32[]{:S(2)}) copy-start(f32[4,8,8,512]{3,2,1,0:T(8,128)} %get-tuple-element.8) | copy-start | bytes 1572868

commit v2 on v1

v2 whole, which is shorter than its diff:
```python
from functools import partial

import jax
import jax.numpy as jnp
import numpy as np
from jax import lax
from jax.experimental import pallas as pl
from jax.experimental.pallas import tpu as pltpu
from jax.sharding import PartitionSpec as P

ITERS = 2
RHO = 16.0
LANES = 128
OUTER = 4


def split(block):
    return ([block[i] for i in range(4)], [block[i + 4] for i in range(4)])


def product(left, right):
    lr, li = left
    rr, ri = right
    out_real, out_imag = [], []
    for row in range(2):
        for col in range(2):
            a, b = 2 * row, 2 * row + 1
            out_real.append(lr[a] * rr[col] - li[a] * ri[col] + lr[b] * rr[col + 2] - li[b] * ri[col + 2])
            out_imag.append(lr[a] * ri[col] + li[a] * rr[col] + lr[b] * ri[col + 2] + li[b] * rr[col + 2])
    return (out_real, out_imag)


def product_right_adjoint(left, right):
    lr, li = left
    rr, ri = right
    out_real, out_imag = [], []
    for row in range(2):
        for col in range(2):
            a, b, c, d = 2 * row, 2 * row + 1, 2 * col, 2 * col + 1
            out_real.append(lr[a] * rr[c] + li[a] * ri[c] + lr[b] * rr[d] + li[b] * ri[d])
            out_imag.append(li[a] * rr[c] - lr[a] * ri[c] + li[b] * rr[d] - lr[b] * ri[d])
    return (out_real, out_imag)


def product_left_adjoint(left, right):
    lr, li = left
    rr, ri = right
    out_real, out_imag = [], []
    for row in range(2):
        for col in range(2):
            a, b, c, d = row, row + 2, col, col + 2
            out_real.append(lr[a] * rr[c] + li[a] * ri[c] + lr[b] * rr[d] + li[b] * ri[d])
            out_imag.append(lr[a] * ri[c] - li[a] * rr[c] + lr[b] * ri[d] - li[b] * rr[d])
    return (out_real, out_imag)


def normal(r, i, rows):
    (a, b), (c, d) = rows
    top = r[a] * r[a] + i[a] * i[a] + r[b] * r[b] + i[b] * i[b]
    bottom = r[c] * r[c] + i[c] * i[c] + r[d] * r[d] + i[d] * i[d]
    real = r[a] * r[c] + i[a] * i[c] + r[b] * r[d] + i[b] * i[d]
    imag = i[a] * r[c] - r[a] * i[c] + i[b] * r[d] - r[b] * i[d]
    return top, bottom, real, imag


def basis_weights(count):
    x = (2.0 * np.arange(count, dtype=np.float64) + 1.0) / count - 1.0
    basis = np.stack([np.ones_like(x), x, 1.5 * x * x - 0.5, 2.5 * x * x * x - 1.5 * x], axis=1)
    return np.linalg.solve(basis.T @ basis, basis.T)


def halves(value):
    high = value.astype(jnp.bfloat16)
    return high, (value - high.astype(jnp.float32)).astype(jnp.bfloat16)


def from_basis(bases, f, coefficients):
    total = coefficients[0]
    for j in range(1, len(coefficients)):
        total = total + bases[f][j] * coefficients[j]
    return total


def local_bases(F, nf):
    bases = []
    for f in range(F):
        channel = (lax.axis_index("freq") * F + f).astype(jnp.float32)
        x = (2.0 * channel + 1.0) / (F * nf) - 1.0
        bases.append([None, x, 1.5 * x * x - 0.5, 2.5 * x * x * x - 1.5 * x])
    return bases


def fit_kernel(cfg, mixed, gains_ref, duals_ref, gains_out, duals_out, poly_out):
    F, K, S, nt, nf, inner, chunks, terms_poly = cfg
    CH = S // chunks
    FK = F * 8 * K
    weights = basis_weights(F * nf)
    bases = local_bases(F, nf)
    gains_out[...] = gains_ref[...]

    def rows(n, chunk, c):
        at = ((n % F) * 8 + c) * K
        return mixed[n // F, chunk, at // (FK // 2), at % (FK // 2) : at % (FK // 2) + K, :]

    for chunk in range(mixed.shape[1]):
        lanes = slice(chunk * CH, (chunk + 1) * CH)
        for c in range(8):
            values = [rows(n, chunk, c) for n in range(nf * F)]
            coefficients = []
            for j in range(terms_poly):
                total = float(weights[j, 0]) * values[0]
                for n in range(1, nf * F):
                    total = total + float(weights[j, n]) * values[n]
                poly_out[j, c, :, lanes] = total
                coefficients.append(total)
            for f in range(F):
                prior = from_basis(bases, f, coefficients)
                duals_out[f, c, :, lanes] = duals_ref[f, c, :, lanes] + RHO * (gains_ref[f, c, :, lanes] - prior)


def kernel(cfg, vis_hbm, coh_hbm, pairs_hbm, gains_hbm, duals_hbm, poly_hbm,
           gains_out, mixed,
           data, hot, terms, jones, taken, vis_ref, coh_ref, pairs_ref, gains_ref, duals_ref, poly_ref,
           tm_send, tm_recv, fq_send, fq_recv, load_sem):
    F, K, S, nt, nf, inner, chunks, terms_poly = cfg
    CH = S // chunks
    FK = F * 8 * K
    tm = lax.axis_index("tm")
    fq = lax.axis_index("freq")
    z, y = tm // inner, tm % inner
    partner = fq + 1 - 2 * (fq % 2)
    mate = tm + 1 - 2 * (tm % 2)
    MESH = pl.DeviceIdType.MESH

    loads = [pltpu.make_async_copy(src, dst, load_sem.at[i]) for i, (src, dst) in enumerate(
        ((gains_hbm, gains_ref), (duals_hbm, duals_ref), (poly_hbm, poly_ref),
         (coh_hbm, coh_ref), (vis_hbm, vis_ref), (pairs_hbm, pairs_ref)))]

    def tm_at(dz, dy):
        return ((z + dz) % OUTER) * inner + (y + dy) % inner

    for load in reversed(loads):
        load.start()
    barrier = pltpu.get_barrier_semaphore()

    def greet(peer):
        pl.semaphore_signal(barrier, inc=1, device_id=peer, device_id_type=MESH)

    peers = [{"tm": tm_at(d, 0)} for d in range(1, OUTER)]
    peers += [{"tm": tm_at(0, e)} for e in range(1, inner)]
    peers += [{"freq": partner}]
    peers += [{"freq": (fq + 2 * d) % nf} for d in range(1, nf // 2)]
    for peer in peers:
        greet(peer)
    for load in loads[3:]:
        load.wait()
    data[tm, 0, 0:2, :] = pairs_ref[...].astype(jnp.float32)
    for f in range(F):
        data[tm, f, 8:16, :] = vis_ref[f]
        data[tm, f, 16:, :] = coh_ref[f].astype(jnp.float32).reshape(8 * K, LANES)

    def load_gains(gains):
        high, low = halves(gains)
        jones[0:FK, :] = high
        jones[FK : 2 * FK, :] = low

    pl.semaphore_wait(barrier, len(peers))

    def tm_copy(block, f, slot, device):
        rows = pl.ds(0, 16 + 8 * K) if f == 0 else pl.ds(8, 8 + 8 * K)
        return pltpu.make_async_remote_copy(
            src_ref=data.at[block, f, rows], dst_ref=data.at[block, f, rows],
            send_sem=tm_send.at[slot, f], recv_sem=tm_recv.at[block, f],
            device_id={"tm": device}, device_id_type=MESH)

    def arrived(block, f):
        tm_copy(block, f, 0, mate).wait_recv()

    sends = []

    def send(block, f, slot, device):
        copy = tm_copy(block, f, slot, device)
        copy.start()
        sends.append(copy)

    def relay(d, f):
        for e in range(1, inner):
            send(tm_at(d, 0), f, OUTER + d * inner + e, tm_at(0, e))

    for f in range(F):
        for d in (1, 3, 2):
            send(tm, f, d, tm_at(d, 0))
        relay(0, f)

    stations = lax.broadcasted_iota(jnp.int32, (S, LANES), 0).astype(jnp.float32)

    def columns(block, half):
        return pl.ds(pl.multiple_of(block * 2 * LANES + half * LANES, LANES), LANES)

    def make_hot(block):
        for half in range(2):
            row = data[block, 0, half : half + 1, :]
            hot[:, columns(block, half)] = jnp.where(stations == row, 1.0, 0.0).astype(jnp.bfloat16)

    def gather(block):
        both = pl.ds(pl.multiple_of(block * 2 * LANES, 2 * LANES), 2 * LANES)
        found = jnp.dot(jones[...], hot[:, both], preferred_element_type=jnp.float32)
        taken[block] = found[:FK] + found[FK:]

    def rows_sums(block, channels):
        for f in channels:
            base = f * 8 * K
            first = split([taken[block, base + c * K : base + (c + 1) * K, :LANES] for c in range(8)])
            second = split([taken[block, base + c * K : base + (c + 1) * K, LANES:] for c in range(8)])
            sky = split([data[block, f, 16 + c * K : 16 + (c + 1) * K, :] for c in range(8)])
            left = product(first, sky)
            right = product_right_adjoint(sky, second)
            model = product_right_adjoint(left, second)
            model = model[0] + model[1]
            residual = []
            for c in range(8):
                seen = data[block, f, 8 + c : 9 + c, :]
                residual.append(jnp.broadcast_to(seen - jnp.sum(model[c], axis=0, keepdims=True), (K, LANES)))
            residual = split(residual)
            ends = []
            out = product_right_adjoint(residual, right)
            ends.append(out[0] + out[1] + list(normal(right[0], right[1], ((0, 1), (2, 3)))))
            out = product_left_adjoint(residual, left)
            top, bottom, real, imag = normal(left[0], left[1], ((0, 2), (1, 3)))
            ends.append(out[0] + out[1] + [top, bottom, real, -imag])
            for half in range(2):
                high, low = halves(jnp.concatenate(ends[half], axis=0))
                terms[f * 12 * K : (f + 1) * 12 * K, columns(block, half)] = high
                terms[(F + f) * 12 * K : (F + f + 1) * 12 * K, columns(block, half)] = low

    bases = local_bases(F, nf)

    def update(source, damping, chunk):
        lanes = slice(chunk * CH, (chunk + 1) * CH)
        sums = lax.dot_general(terms[...], hot[lanes, :], (((1,), (1,)), ((), ())),
                               preferred_element_type=jnp.float32)
        half = F * 12 * K
        sums = sums[:half] + sums[half:]
        for f in range(F):
            part = [sums[(f * 12 + c) * K : (f * 12 + c + 1) * K] for c in range(12)]
            old, step = [], []
            for c in range(8):
                prior = from_basis(bases, f, [poly_ref[j, c, :, lanes] for j in range(terms_poly)])
                gain = source[f, c, :, lanes]
                old.append(gain)
                step.append(part[c] - duals_ref[f, c, :, lanes] - RHO * (gain - prior))
            top, bottom, real, imag = part[8:]
            shift = damping * 0.5 * (top + bottom) + RHO
            upper, lower = top + shift, bottom + shift
            scale = 1.0 / (upper * lower - real * real - imag * imag)
            a, d, br, bi = lower * scale, upper * scale, -real * scale, -imag * scale
            sr, si = split(step)
            for row in range(2):
                p, q = 2 * row, 2 * row + 1
                gains_out[f, p, :, lanes] = old[p] + sr[p] * a + sr[q] * br + si[q] * bi
                gains_out[f, p + 4, :, lanes] = old[p + 4] + si[p] * a + si[q] * br - sr[q] * bi
                gains_out[f, q, :, lanes] = old[q] + sr[p] * br - si[p] * bi + sr[q] * d
                gains_out[f, q + 4, :, lanes] = old[q + 4] + si[p] * br + sr[p] * bi + si[q] * d

    def take(block, f):
        if f == 0:
            make_hot(block)
            gather(block)
        rows_sums(block, [f])

    loads[0].wait()
    load_gains(gains_ref[...].reshape(FK, S))
    for f in range(F):
        take(tm, f)
    for f in range(F):
        for d in (1, 3):
            arrived(tm_at(d, 0), f)
            relay(d, f)
    for e in range(1, inner):
        for f in range(F):
            arrived(tm_at(0, e), f)
            take(tm_at(0, e), f)
    for f in range(F):
        arrived(tm_at(2, 0), f)
        relay(2, f)
    for d in (1, 3, 2):
        for f in range(F):
            take(tm_at(d, 0), f)
    for d in (1, 3, 2):
        for e in range(1, inner):
            for f in range(F):
                arrived(tm_at(d, e), f)
                take(tm_at(d, e), f)

    loads[1].wait()
    loads[2].wait()
    for chunk in range(chunks):
        update(gains_ref, 12.0, chunk)
    for inner_step in range(1, ITERS):
        load_gains(gains_out[...].reshape(FK, S))

        @pl.loop(0, nt)
        def _(block):
            gather(block)
            rows_sums(block, range(F))

        if inner_step < ITERS - 1:
            for chunk in range(chunks):
                update(gains_out, 12.0 * 0.5**inner_step, chunk)

    def fq_copy(owner, chunk, slot, device):
        return pltpu.make_async_remote_copy(
            src_ref=mixed.at[owner, chunk], dst_ref=mixed.at[owner, chunk],
            send_sem=fq_send.at[slot, chunk], recv_sem=fq_recv.at[owner, chunk],
            device_id={"freq": device}, device_id_type=MESH)

    fq_sends = []

    def fq_start(owner, chunk, slot, device):
        copy = fq_copy(owner, chunk, slot, device)
        copy.start()
        fq_sends.append(copy)

    others = nf // 2
    for chunk in range(chunks):
        lanes = slice(chunk * CH, (chunk + 1) * CH)
        update(gains_out, 12.0 * 0.5 ** (ITERS - 1), chunk)
        value = gains_out[:, :, :, lanes] + duals_ref[:, :, :, lanes] * (1.0 / RHO)
        mixed[fq, chunk] = value.reshape(2, FK // 2, CH)
        for d in range(1, others):
            fq_start(fq, chunk, d, (fq + 2 * d) % nf)
        fq_start(fq, chunk, 0, partner)

    for chunk in range(chunks):
        for d in range(1, others):
            owner = (fq - 2 * d + nf) % nf
            fq_copy(owner, chunk, 0, partner).wait_recv()
            fq_start(owner, chunk, others + d, partner)
    for chunk in range(chunks):
        fq_copy(partner, chunk, 0, partner).wait_recv()
        for d in range(1, others):
            fq_copy((partner - 2 * d + nf) % nf, chunk, 0, partner).wait_recv()
    for copy in sends + fq_sends:
        copy.wait_send()


def solution(mesh):
    nt, nf = mesh.shape["tm"], mesh.shape["freq"]

    def shards(visibilities, coherencies, pairs, gains_start, duals_start, poly_start):
        F, _, K, S = gains_start.shape
        inner = nt // OUTER
        chunks = 2
        FK = F * 8 * K
        CH = S // chunks
        cfg = (F, K, S, nt, nf, inner, chunks, poly_start.shape[0])
        like = lambda x: jax.ShapeDtypeStruct(x.shape, jnp.float32)
        vmem = pl.BlockSpec(memory_space=pltpu.VMEM)
        hbm = pl.BlockSpec(memory_space=pltpu.HBM)
        gains, mixed = pl.pallas_call(
            partial(kernel, cfg),
            out_shape=(like(gains_start), jax.ShapeDtypeStruct((nf, chunks, 2, FK // 2, CH), jnp.float32)),
            in_specs=[hbm] * 6,
            out_specs=(vmem,) * 2,
            scratch_shapes=[
                pltpu.VMEM((nt, F, 16 + 8 * K, LANES), jnp.float32),
                pltpu.VMEM((S, nt * 2 * LANES), jnp.bfloat16),
                pltpu.VMEM((2 * F * 12 * K, nt * 2 * LANES), jnp.bfloat16),
                pltpu.VMEM((2 * FK, S), jnp.bfloat16),
                pltpu.VMEM((nt, FK, 2 * LANES), jnp.float32),
                pltpu.VMEM(visibilities.shape, jnp.float32),
                pltpu.VMEM(coherencies.shape, jnp.bfloat16),
                pltpu.VMEM(pairs.shape, jnp.int32),
                pltpu.VMEM(gains_start.shape, jnp.float32),
                pltpu.VMEM(gains_start.shape, jnp.float32),
                pltpu.VMEM(poly_start.shape, jnp.float32),
                pltpu.SemaphoreType.DMA((OUTER + OUTER * inner, F)),
                pltpu.SemaphoreType.DMA((nt, F)),
                pltpu.SemaphoreType.DMA((nf + 1, chunks)),
                pltpu.SemaphoreType.DMA((nf, chunks)),
                pltpu.SemaphoreType.DMA((6,)),
            ],
            compiler_params=pltpu.CompilerParams(collective_id=0, has_side_effects=True,
                                                 vmem_limit_bytes=58 * 2**20),
        )(visibilities, coherencies, pairs, gains_start, duals_start, poly_start)
        own = pl.BlockSpec((F, 8, K, CH), lambda i: (0, 0, 0, i))
        return pl.pallas_call(
            partial(fit_kernel, cfg),
            grid=(chunks,),
            out_shape=(like(gains_start), like(duals_start), like(poly_start)),
            in_specs=[pl.BlockSpec((nf, 1, 2, FK // 2, CH), lambda i: (0, i, 0, 0, 0)), own, own],
            out_specs=(own, own, pl.BlockSpec((poly_start.shape[0], 8, K, CH), lambda i: (0, 0, 0, i))),
            compiler_params=pltpu.CompilerParams(vmem_limit_bytes=60 * 2**20),
        )(mixed, gains, duals_start)

    placed = (
        P("freq", None, "tm"),
        P("freq", None, None, "tm"),
        P(None, "tm"),
        P("freq", None, None, None),
        P("freq", None, None, None),
        P(),
    )
    return jax.shard_map(
        shards,
        mesh=mesh,
        in_specs=placed,
        out_specs=(P("freq", None, None, None), P("freq", None, None, None), P()),
        check_vma=False,
    )
```

time: 36.7 us -> 33.6 us (0.916)
  local copies, waits for them, and re-layouts: 3.25 us -> 0 us
    unnamed x7 -> x0, local copies, waits for them, and re-layouts: 3.25 us -> none
    pallas_call x1 -> x2, Pallas kernels: 32.5 us -> 32.8 us  [the longest x1 30.5 us: shards(): pl.pallas_call(partial(kernel, cfg), out_shape=(like(gains_start), jax.Sh...]
where the time goes in v2:
time: 33.6 us; the launch traced here: 33.4 us
  Pallas kernels  32.8 us (98%)
  between operations  0.64 us (2%)
    pallas_call x1, Pallas kernels, shards(): pl.pallas_call(partial(kernel, cfg), out_shape=(like(gains_start), jax.Sh...  30.5 us
    pallas_call x1, Pallas kernels, shards(): pl.pallas_call(partial(fit_kernel, cfg), grid=(chunks,), out_shape=(like(...  2.3 us

profile of v2, /device:TPU:0, one launch (start us, length us, event | category | flops | bytes accessed | tf_op | source)
XLA Modules:
  0.0 33.4 jit_solution(3630938247804802843)
XLA Ops:
  0.6 30.5 %shard_map.85 = (f32[2,8,8,512]{3,2,1,0:T(8,128)}, f32[4,2,2,64,256]{4,3,2,1,0:T(8,128)}) custom-call(f32[2,8,128]{2,1,0:T(8,128)} %vis_hbm.1, bf16[2,8,8,128]{3,2,1,0:T(8,128)(2,1)} %coh_hbm.1, s32[2,128]{1,0:T(2,128)} %pairs_hbm.1, f32[2,8,8,512]{3,2,1,0:T(8,128)} %gains_hbm.1, f32[2,8,8,512]{3,2,1,0:T(8,128)} %duals_ref.1, f32[4,8,8,512]{3,2,1,0:T(8,128)} %poly_hbm.1), custom_call_target="tpu_custom_call" | custom-call | tf_op jit(solution)/shard_map/pallas_call | solution.py:360
  31.1 2.3 %shard_map.86 = (f32[2,8,8,512]{3,2,1,0:T(8,128)}, f32[2,8,8,512]{3,2,1,0:T(8,128)}, f32[4,8,8,512]{3,2,1,0:T(8,128)}) custom-call(f32[4,2,2,64,256]{4,3,2,1,0:T(8,128)} %get-tuple-element.5.mixed, f32[2,8,8,512]{3,2,1,0:T(8,128)} %get-tuple-element.6.gains_ref, f32[2,8,8,512]{3,2,1,0:T(8,128)} %duals_ref.1), custom_call_target="tpu_custom_call" | custom-call | tf_op jit(solution)/shard_map/pallas_call | solution.py:387

commit v3 on v2

--- a/solution.py
+++ b/solution.py
@@ -235,8 +235,7 @@
 
     bases = local_bases(F, nf)
 
-    def update(source, damping, chunk):
-        lanes = slice(chunk * CH, (chunk + 1) * CH)
+    def update(source, damping, lanes):
         sums = lax.dot_general(terms[...], hot[lanes, :], (((1,), (1,)), ((), ())),
                                preferred_element_type=jnp.float32)
         half = F * 12 * K
@@ -294,8 +293,7 @@
 
     loads[1].wait()
     loads[2].wait()
-    for chunk in range(chunks):
-        update(gains_ref, 12.0, chunk)
+    update(gains_ref, 12.0, slice(0, S))
     for inner_step in range(1, ITERS):
         load_gains(gains_out[...].reshape(FK, S))
 
@@ -305,8 +303,7 @@
             rows_sums(block, range(F))
 
         if inner_step < ITERS - 1:
-            for chunk in range(chunks):
-                update(gains_out, 12.0 * 0.5**inner_step, chunk)
+            update(gains_out, 12.0 * 0.5**inner_step, slice(0, S))
 
     def fq_copy(owner, chunk, slot, device):
         return pltpu.make_async_remote_copy(
@@ -324,7 +321,7 @@
     others = nf // 2
     for chunk in range(chunks):
         lanes = slice(chunk * CH, (chunk + 1) * CH)
-        update(gains_out, 12.0 * 0.5 ** (ITERS - 1), chunk)
+        update(gains_out, 12.0 * 0.5 ** (ITERS - 1), lanes)
         value = gains_out[:, :, :, lanes] + duals_ref[:, :, :, lanes] * (1.0 / RHO)
         mixed[fq, chunk] = value.reshape(2, FK // 2, CH)
         for d in range(1, others):

time: 33.6 us -> 33.6 us (level)
  no operation moved by 1% of the time
where the time goes in v3:
time: 33.6 us; the launch traced here: 33.4 us
  Pallas kernels  32.8 us (98%)
  between operations  0.64 us (2%)
    pallas_call x1, Pallas kernels, shards(): pl.pallas_call(partial(kernel, cfg), out_shape=(like(gains_start), jax.Sh...  30.5 us
    pallas_call x1, Pallas kernels, shards(): pl.pallas_call(partial(fit_kernel, cfg), grid=(chunks,), out_shape=(like(...  2.3 us

profile of v3, /device:TPU:0, one launch (start us, length us, event | category | flops | bytes accessed | tf_op | source)
XLA Modules:
  0.0 33.4 jit_solution(12029589322828838436)
XLA Ops:
  0.6 30.5 %shard_map.85 = (f32[2,8,8,512]{3,2,1,0:T(8,128)}, f32[4,2,2,64,256]{4,3,2,1,0:T(8,128)}) custom-call(f32[2,8,128]{2,1,0:T(8,128)} %vis_hbm.1, bf16[2,8,8,128]{3,2,1,0:T(8,128)(2,1)} %coh_hbm.1, s32[2,128]{1,0:T(2,128)} %pairs_hbm.1, f32[2,8,8,512]{3,2,1,0:T(8,128)} %gains_hbm.1, f32[2,8,8,512]{3,2,1,0:T(8,128)} %duals_ref.1, f32[4,8,8,512]{3,2,1,0:T(8,128)} %poly_hbm.1), custom_call_target="tpu_custom_call" | custom-call | tf_op jit(solution)/shard_map/pallas_call | solution.py:357
  31.1 2.3 %shard_map.86 = (f32[2,8,8,512]{3,2,1,0:T(8,128)}, f32[2,8,8,512]{3,2,1,0:T(8,128)}, f32[4,8,8,512]{3,2,1,0:T(8,128)}) custom-call(f32[4,2,2,64,256]{4,3,2,1,0:T(8,128)} %get-tuple-element.5.mixed, f32[2,8,8,512]{3,2,1,0:T(8,128)} %get-tuple-element.6.gains_ref, f32[2,8,8,512]{3,2,1,0:T(8,128)} %duals_ref.1), custom_call_target="tpu_custom_call" | custom-call | tf_op jit(solution)/shard_map/pallas_call | solution.py:384
